TPU v7x, 32 devices: a whole 2x2x4 slice. The times are simulated.
32 devices in a mesh: dp: 4 (over y, core), row: 2 (over x), col: 4 (over z).
Axes of the slice: x: 2, y: 2, z: 4, core: 2. Of those that a mesh axis runs over, the one named last changes fastest.
Arguments:
- layer_input: bfloat16 [12288, 1536], P(('dp', 'col'), 'row'), may hold values from -6 to 6
- attn_gain: float32 [1536], P('row'), may hold values from 0.25 to 1.75
- qkv_weight: bfloat16 [1536, 4608], P('row', 'col'), may hold values from -0.15625 to 0.15625
- forget_weight: bfloat16 [1536, 24], P('row', 'col'), may hold values from -0.15625 to 0.15625
- forget_bias: float32 [24], P('col'), may hold values from 2.5 to 7
- out_weight: bfloat16 [1536, 1536], P('col', 'row'), may hold values from -0.625 to 0.625
- ffn_gain: float32 [1536], P('row'), may hold values from 0.25 to 1.75
- gate_weight: bfloat16 [1536, 4096], P('row', 'col'), may hold values from -0.15625 to 0.15625
- up_weight: bfloat16 [1536, 4096], P('row', 'col'), may hold values from -0.15625 to 0.15625
- down_weight: bfloat16 [4096, 1536], P('col', 'row'), may hold values from -0.09375 to 0.09375
- prompt_doc: int32 [8, 1024], P(('dp', 'row')), may hold values from 0 to 3, never falling along the last dimension, each value on 1 to 512 neighbouring positions
- branch_seg: int32 [8, 512], P(('dp', 'row')), may hold values from 0 to 3, never falling along the last dimension, each value on 1 to 256 neighbouring positions
- branch_doc: int32 [8, 4], P(('dp', 'row')), may hold values from 0 to 3
- out_cotangent: bfloat16 [12288, 1536], P(('dp', 'col'), 'row'), may hold values from -6 to 6
Outputs:
- layer_output: bfloat16 [12288, 1536], P(('dp', 'col'), 'row')
- input_grad: bfloat16 [12288, 1536], P(('dp', 'col'), 'row')
- attn_gain_grad: float32 [1536], P('row')
- qkv_grad: float32 [1536, 4608], P('row', 'col')
- forget_grad: float32 [1536, 24], P('row', 'col')
- forget_bias_grad: float32 [24], P('col')
- out_grad: float32 [1536, 1536], P('col', 'row')
- ffn_gain_grad: float32 [1536], P('row')
- gate_grad: float32 [1536, 4096], P('row', 'col')
- up_grad: float32 [1536, 4096], P('row', 'col')
- down_grad: float32 [4096, 1536], P('col', 'row')
Inputs may be any that keep to these rules, and one draw needn't show every extreme that they name: `prompt_doc`: in each group the prompt's documents are numbered 0 to 3 in order, every one present, each of 1 to 512 tokens, one of exactly 512. `branch_seg`: in each group the continuations are numbered 0 to 3 in order, every one present, each of 1 to 256 tokens, one of exactly 256.
All inputs are finite; a program needn't handle non-finite values.
Results may differ from a plain program's by a relative error of at most 0.023.
Values may be sent and summed in bfloat16 or wider, within the bound.
A program may use at most 192 MiB of HBM per device.

v0:
```python
import jax
import jax.numpy as jnp
from jax import lax
from jax.sharding import PartitionSpec as P

D = 1536
DH = 64
DOCS = 4
QBLK = 512
EPS = 1e-06
MASKED = -1e30


def visible(row_start, doc_query, branch_query, doc_key, branch_key):
    pos_query = row_start + jnp.arange(doc_query.shape[0], dtype=jnp.int32)
    pos_key = jnp.arange(doc_key.shape[0], dtype=jnp.int32)
    causal = pos_key[None, :] <= pos_query[:, None]
    same_doc = doc_query[:, None] == doc_key[None, :]
    same_branch = (branch_key[None, :] < 0) | (branch_query[:, None] == branch_key[None, :])
    return causal & same_doc & same_branch


def decay_sums(log_rates, prompt_ids, branch_ids, branch_docs):
    prompt_len = prompt_ids.shape[0]
    prompt_part = log_rates[:prompt_len]
    branch_part = log_rates[prompt_len:]
    prompt_sums = jnp.cumsum(prompt_part, axis=0)
    doc_range = jnp.arange(DOCS, dtype=jnp.int32)
    doc_last = jnp.sum((prompt_ids[None, :] <= doc_range[:, None]).astype(jnp.int32), axis=1) - 1
    at_last = jnp.arange(prompt_len, dtype=jnp.int32)[None, :] == doc_last[:, None]
    doc_totals = jnp.sum(jnp.where(at_last[:, :, None], prompt_sums[None], 0.0), axis=1)
    branch_range = jnp.arange(branch_docs.shape[0], dtype=jnp.int32)
    picked = branch_docs[:, None] == doc_range[None, :]
    branch_start = jnp.sum(jnp.where(picked[:, :, None], doc_totals[None], 0.0), axis=1)
    earlier = branch_ids[None, :] < branch_range[:, None]
    skipped = jnp.sum(jnp.where(earlier[:, :, None], branch_part[None], 0.0), axis=1)
    member = branch_ids[:, None] == branch_range[None, :]
    offsets = jnp.sum(jnp.where(member[:, :, None], (branch_start - skipped)[None], 0.0), axis=1)
    decay_sum = jnp.concatenate([prompt_sums, jnp.cumsum(branch_part, axis=0) + offsets], axis=0)
    branch_doc_ids = jnp.sum(jnp.where(member, branch_docs[None, :], 0), axis=1)
    doc_ids = jnp.concatenate([prompt_ids, branch_doc_ids])
    branch_tags = jnp.concatenate([jnp.full((prompt_len,), -1, jnp.int32), branch_ids])
    return (decay_sum, doc_ids, branch_tags)


def block_scores(query_block, key_rows, decay_query, decay_key, allowed):
    raw_scores = jnp.einsum(
        "qhd,khd->hqk", query_block, key_rows, preferred_element_type=jnp.float32
    )
    scores = raw_scores * DH ** (-0.5) + decay_query.T[:, :, None] - decay_key.T[:, None, :]
    return jnp.where(allowed[None], scores, MASKED)


def contract_rows(left, right):
    return lax.dot_general(
        left, right, (((0,), (0,)), ((), ())), preferred_element_type=jnp.float32
    )


def contract_cols(left, right):
    return lax.dot_general(
        left, right, (((1,), (1,)), ((), ())), preferred_element_type=jnp.float32
    )


def row_stat(values):
    return lax.psum(values, "row")


def gather_tokens(token_rows):
    return lax.all_gather(token_rows, "col", axis=0, tiled=True)


def sum_tokens(partial_value):
    return lax.psum_scatter(
        partial_value.astype(jnp.bfloat16), "col", scatter_dimension=0, tiled=True
    ).astype(jnp.float32)


def gather_group(group_rows):
    return lax.all_gather(group_rows, "row", axis=0, tiled=True)


def sum_group(partial_value):
    return lax.psum_scatter(
        partial_value.astype(jnp.bfloat16), "row", scatter_dimension=0, tiled=True
    ).astype(jnp.float32)


def sum_pair(first, second):
    return (
        lax.psum_scatter(first, "row", scatter_dimension=0, tiled=True),
        lax.psum_scatter(second, "row", scatter_dimension=0, tiled=True),
    )


def gather_pair(first, second):
    return (
        lax.all_gather(first, "row", axis=0, tiled=True),
        lax.all_gather(second, "row", axis=0, tiled=True),
    )


def shards(
    layer_input,
    attn_gain,
    qkv_weight,
    forget_weight,
    forget_bias,
    out_weight,
    ffn_gain,
    gate_weight,
    up_weight,
    down_weight,
    prompt_doc,
    branch_seg,
    branch_doc,
    out_cotangent,
):
    score_scale = DH ** (-0.5)
    stream = layer_input.astype(jnp.float32)
    rms_a = lax.rsqrt(row_stat(jnp.sum(stream * stream, axis=1)) / D + EPS)[:, None]
    normed_a = (stream * rms_a * attn_gain).astype(jnp.bfloat16)
    normed_a_all = gather_tokens(normed_a)
    projected, forget_sum = sum_pair(
        jnp.dot(normed_a_all, qkv_weight, preferred_element_type=jnp.float32),
        jnp.dot(normed_a_all, forget_weight, preferred_element_type=jnp.float32),
    )
    group_len = projected.shape[0]
    heads = forget_weight.shape[1]
    qkv = projected.astype(jnp.bfloat16).reshape(group_len, heads, 3, DH)
    forget_logit = forget_sum + forget_bias
    log_rate = jax.nn.log_sigmoid(forget_logit)
    prompt_ids = prompt_doc[0]
    branch_ids = branch_seg[0]
    branch_docs = branch_doc[0]
    decay_sum, doc_ids, branch_tags = decay_sums(log_rate, prompt_ids, branch_ids, branch_docs)
    queries = qkv[:, :, 0]
    key_rows = qkv[:, :, 1]
    value_rows = qkv[:, :, 2]
    blocks = jnp.arange(group_len // QBLK, dtype=jnp.int32)

    def block_view(block_index):
        row_start = block_index * QBLK
        query_block = lax.dynamic_slice_in_dim(queries, row_start, QBLK, 0)
        decay_query = lax.dynamic_slice_in_dim(decay_sum, row_start, QBLK, 0)
        doc_query = lax.dynamic_slice_in_dim(doc_ids, row_start, QBLK, 0)
        branch_query = lax.dynamic_slice_in_dim(branch_tags, row_start, QBLK, 0)
        allowed = visible(row_start, doc_query, branch_query, doc_ids, branch_tags)
        scores = block_scores(query_block, key_rows, decay_query, decay_sum, allowed)
        return (row_start, query_block, scores)

    def forward_block(block_index):
        row_start, query_block, scores = block_view(block_index)
        row_max = jnp.max(scores, axis=2, keepdims=True)
        expo = jnp.exp(scores - row_max)
        row_total = jnp.sum(expo, axis=2, keepdims=True)
        probs = (expo / row_total).astype(jnp.bfloat16)
        attended_block = jnp.einsum(
            "hqk,khd->qhd", probs, value_rows, preferred_element_type=jnp.float32
        ).astype(jnp.bfloat16)
        return (attended_block, (row_max + jnp.log(row_total))[:, :, 0])

    attended_blocks, lse_blocks = lax.map(forward_block, blocks)
    attended = attended_blocks.reshape(group_len, heads * DH)
    attended_all = gather_group(attended)
    branch_out = sum_tokens(jnp.dot(attended_all, out_weight, preferred_element_type=jnp.float32))
    resid = stream + branch_out
    rms_b = lax.rsqrt(row_stat(jnp.sum(resid * resid, axis=1)) / D + EPS)[:, None]
    normed_b = (resid * rms_b * ffn_gain).astype(jnp.bfloat16)
    normed_b_all = gather_tokens(normed_b)
    gate_pre, up_pre = sum_pair(
        jnp.dot(normed_b_all, gate_weight, preferred_element_type=jnp.float32),
        jnp.dot(normed_b_all, up_weight, preferred_element_type=jnp.float32),
    )
    gate_sig = jax.nn.sigmoid(gate_pre)
    gate_act = gate_pre * gate_sig
    hidden = (gate_act * up_pre).astype(jnp.bfloat16)
    hidden_all = gather_group(hidden)
    layer_output = (
        resid + sum_tokens(jnp.dot(hidden_all, down_weight, preferred_element_type=jnp.float32))
    ).astype(jnp.bfloat16)
    cotangent = out_cotangent.astype(jnp.float32)
    cotangent_all = gather_tokens(out_cotangent)
    down_grad = contract_rows(hidden_all, cotangent_all)
    grad_hidden = sum_group(contract_cols(cotangent_all, down_weight))
    grad_gate = (grad_hidden * up_pre * gate_sig * (1.0 + gate_pre * (1.0 - gate_sig))).astype(
        jnp.bfloat16
    )
    grad_up = (grad_hidden * gate_act).astype(jnp.bfloat16)
    grad_gate_all, grad_up_all = gather_pair(grad_gate, grad_up)
    gate_grad = contract_rows(normed_b_all, grad_gate_all)
    up_grad = contract_rows(normed_b_all, grad_up_all)
    grad_normed_b = sum_tokens(
        contract_cols(grad_gate_all, gate_weight) + contract_cols(grad_up_all, up_weight)
    )
    gained_b = ffn_gain * grad_normed_b
    inner_b = row_stat(jnp.sum(resid * gained_b, axis=1))[:, None]
    ffn_gain_part = jnp.sum(grad_normed_b * resid * rms_b, axis=0)
    grad_resid = cotangent + rms_b * gained_b - resid * (rms_b * rms_b * rms_b) * inner_b / D
    grad_branch = grad_resid.astype(jnp.bfloat16)
    grad_branch_all = gather_tokens(grad_branch)
    out_grad = contract_rows(attended_all, grad_branch_all)
    attended_part = contract_cols(grad_branch_all, out_weight)
    grad_attended = sum_group(attended_part).astype(jnp.bfloat16).reshape(group_len, heads, DH)

    def back_block(carry, block_index):
        key_acc, value_acc, decay_keys = carry
        row_start, query_block, scores = block_view(block_index)
        grad_block = lax.dynamic_slice_in_dim(grad_attended, row_start, QBLK, 0)
        lse_block = lax.dynamic_index_in_dim(lse_blocks, block_index, 0, keepdims=False)
        probs_star = jnp.exp(scores - lse_block[:, :, None])
        grad_probs = jnp.einsum(
            "qhd,khd->hqk", grad_block, value_rows, preferred_element_type=jnp.float32
        )
        row_delta = jnp.sum(probs_star * grad_probs, axis=2, keepdims=True)
        grad_scores = (probs_star * (grad_probs - row_delta)).astype(jnp.bfloat16)
        grad_query = (
            jnp.einsum("hqk,khd->qhd", grad_scores, key_rows, preferred_element_type=jnp.float32)
            * score_scale
        )
        key_acc = key_acc + jnp.einsum(
            "hqk,qhd->khd", grad_scores, query_block, preferred_element_type=jnp.float32
        )
        value_acc = value_acc + jnp.einsum(
            "hqk,qhd->khd",
            probs_star.astype(jnp.bfloat16),
            grad_block,
            preferred_element_type=jnp.float32,
        )
        decay_rows = jnp.sum(grad_scores, axis=2, dtype=jnp.float32)
        decay_keys = decay_keys - jnp.sum(grad_scores, axis=1, dtype=jnp.float32)
        return ((key_acc, value_acc, decay_keys), (grad_query, decay_rows))

    zero_rows = jnp.zeros((group_len, heads, DH), jnp.float32)
    carried, stacked = lax.scan(
        back_block, (zero_rows, zero_rows, jnp.zeros((heads, group_len), jnp.float32)), blocks
    )
    key_acc, value_acc, decay_keys = carried
    query_blocks, decay_blocks = stacked
    grad_query = query_blocks.reshape(group_len, heads, DH)
    grad_decay = jnp.transpose(decay_blocks, (0, 2, 1)).reshape(group_len, heads) + decay_keys.T
    grad_qkv = (
        jnp.stack([grad_query, key_acc * score_scale, value_acc], axis=2)
        .astype(jnp.bfloat16)
        .reshape(group_len, heads * 3 * DH)
    )
    unused, pullback = jax.vjp(
        lambda log_rates: decay_sums(log_rates, prompt_ids, branch_ids, branch_docs)[0], log_rate
    )
    grad_log_rate = pullback(grad_decay)[0]
    grad_forget = (grad_log_rate * jax.nn.sigmoid(-forget_logit)).astype(jnp.bfloat16)
    grad_qkv_all, grad_forget_all = gather_pair(grad_qkv, grad_forget)
    qkv_grad = contract_rows(normed_a_all, grad_qkv_all)
    forget_grad = contract_rows(normed_a_all, grad_forget_all)
    forget_bias_grad = jnp.sum(grad_forget_all, axis=0, dtype=jnp.float32)
    grad_normed_a = sum_tokens(
        contract_cols(grad_qkv_all, qkv_weight) + contract_cols(grad_forget_all, forget_weight)
    )
    gained_a = attn_gain * grad_normed_a
    inner_a = row_stat(jnp.sum(stream * gained_a, axis=1))[:, None]
    attn_gain_part = jnp.sum(grad_normed_a * stream * rms_a, axis=0)
    input_grad = (
        grad_resid + rms_a * gained_a - stream * (rms_a * rms_a * rms_a) * inner_a / D
    ).astype(jnp.bfloat16)
    attn_gain_grad, ffn_gain_grad = lax.psum((attn_gain_part, ffn_gain_part), ("dp", "col"))
    summed = (
        lax.psum(qkv_grad.astype(jnp.bfloat16), "dp").astype(jnp.float32),
        lax.psum(forget_grad.astype(jnp.bfloat16), "dp").astype(jnp.float32),
        lax.psum(forget_bias_grad.astype(jnp.bfloat16), "dp").astype(jnp.float32),
        lax.psum(out_grad.astype(jnp.bfloat16), "dp").astype(jnp.float32),
        lax.psum(gate_grad.astype(jnp.bfloat16), "dp").astype(jnp.float32),
        lax.psum(up_grad.astype(jnp.bfloat16), "dp").astype(jnp.float32),
        lax.psum(down_grad.astype(jnp.bfloat16), "dp").astype(jnp.float32),
    )
    return (
        layer_output,
        input_grad,
        attn_gain_grad,
        summed[0],
        summed[1],
        summed[2],
        summed[3],
        ffn_gain_grad,
        summed[4],
        summed[5],
        summed[6],
    )


def solution(mesh):
    in_specs = (
        P(("dp", "col"), "row"),
        P("row"),
        P("row", "col"),
        P("row", "col"),
        P("col"),
        P("col", "row"),
        P("row"),
        P("row", "col"),
        P("row", "col"),
        P("col", "row"),
        P(("dp", "row"), None),
        P(("dp", "row"), None),
        P(("dp", "row"), None),
        P(("dp", "col"), "row"),
    )
    out_specs = (
        P(("dp", "col"), "row"),
        P(("dp", "col"), "row"),
        P("row"),
        P("row", "col"),
        P("row", "col"),
        P("col"),
        P("col", "row"),
        P("row"),
        P("row", "col"),
        P("row", "col"),
        P("col", "row"),
    )
    return jax.shard_map(shards, mesh=mesh, in_specs=in_specs, out_specs=out_specs, check_vma=False)
```

profile of v0, /device:TPU:0, one launch (start us, length us, event | category | flops | bytes accessed | tf_op | source)
XLA Modules:
  0.0 2115.4 jit_solution(11031045359977941894)
XLA Ops:
  8.9 5.8 psum.91
  18.7 91.3 %all-gather.10.cloned.1.call-done = bf16[3072,768]{1,0:T(8,128)(2,1)} async-done(((bf16[768,768]{1,0:T(8,128)(2,1)}), bf16[3072,768]{1,0:T(8,128)(2,1)}) %all-gather.10.cloned.1.call-update) | async-done | bytes 4718608 | tf_op jit(solution)/shard_map/all_gather | solution.py:71
  114.4 11.1 fusion.65
  132.6 154.2 %reduce-scatter.11.cloned.1.call-done = f32[1536,1152]{1,0:T(8,128)} async-done(((f32[3072,1152]{1,0:T(8,128)}), f32[1536,1152]{1,0:T(8,128)}) %reduce-scatter.11.cloned.1.call-update) | async-done | bytes 7077904 | tf_op jit(solution)/shard_map/reduce_scatter | solution.py:92
  286.8 5.2 convert_element_type.142
  292.0 5.7 copy.48
  301.6 77.2 %while.31 = (s32[]{:T(128)}, bf16[3,512,6,64]{1,3,2,0:T(8,128)(2,1)}, f32[3,6,512]{2,1,0:T(8,128)S(1)}, s32[3]{0:T(128)S(1)}, s32[1536]{0:T(1024)S(1)}, /*index=...) while((s32[]{:T(128)}, ...), condition=%wide.region_17.18_spmd, body=%wide.region_14.17_spmd.sunk | while | flops 1297808384 | bytes 66381052 | solution.py:164
  304.7 7.2 fusion.137
  311.9 6.5 fusion.138
  318.5 8.9 fusion.139
  330.3 7.2 fusion.137
  337.5 6.5 fusion.138
  344.1 8.9 fusion.139
  355.9 7.2 fusion.137
  363.1 6.5 fusion.138
  369.7 8.9 fusion.139
  382.5 36.2 %all-gather.12.cloned.1.call-done = bf16[3072,384]{0,1:T(8,128)(2,1)} async-done(((bf16[1536,384]{0,1:T(8,128)(2,1)}), bf16[3072,384]{0,1:T(8,128)(2,1)}) %all-gather.12.cloned.1.call-update) | async-done | bytes 2359312 | tf_op jit(solution)/shard_map/all_gather | solution.py:81
  418.7 6.4 convolution_convert_fusion.2
  425.8 84.8 %reduce-scatter.15.cloned.1.call-done = bf16[768,768]{1,0:T(8,128)(2,1)} async-done(((bf16[3072,768]{1,0:T(8,128)(2,1)}), bf16[768,768]{1,0:T(8,128)(2,1)}) %reduce-scatter.15.cloned.1.call-update) | async-done | bytes 1179664 | tf_op jit(solution)/shard_map/reduce_scatter | solution.py:75
  520.1 81.9 %all-gather.18.cloned.1.call-done = bf16[3072,768]{1,0:T(8,128)(2,1)} async-done(((bf16[768,768]{1,0:T(8,128)(2,1)}), bf16[3072,768]{1,0:T(8,128)(2,1)}) %all-gather.18.cloned.1.call-update) | async-done | bytes 4718608 | tf_op jit(solution)/shard_map/all_gather | solution.py:71
  602.0 9.7 convolution_convert_fusion
  611.7 80.3 %all-gather.14.cloned.1.call-done = bf16[3072,768]{1,0:T(8,128)(2,1)} async-done(((bf16[768,768]{1,0:T(8,128)(2,1)}), bf16[3072,768]{1,0:T(8,128)(2,1)}) %all-gather.14.cloned.1.call-update) | async-done | bytes 4718608 | tf_op jit(solution)/shard_map/all_gather | solution.py:71
  692.0 10.0 fusion.68
  702.1 10.4 fusion.67
  712.6 57.2 %reduce-scatter.23.cloned.1.call-done = bf16[1536,1024]{1,0:T(8,128)(2,1)} async-done(((bf16[3072,1024]{1,0:T(8,128)(2,1)}), bf16[1536,1024]{1,0:T(8,128)(2,1)}) %reduce-scatter.23.cloned.1.call-update) | async-done | bytes 3145744 | tf_op jit(solution)/shard_map/reduce_scatter | solution.py:85
  769.9 146.9 %reduce-scatter.19.cloned.1.call-done = f32[1536,1024]{1,0:T(8,128)} async-done(((f32[3072,1024]{1,0:T(8,128)}), f32[1536,1024]{1,0:T(8,128)}) %reduce-scatter.19.cloned.1.call-update) | async-done | bytes 6291472 | tf_op jit(solution)/shard_map/reduce_scatter | solution.py:93
  916.8 146.7 %reduce-scatter.17.cloned.1.call-done = f32[1536,1024]{1,0:T(8,128)} async-done(((f32[3072,1024]{1,0:T(8,128)}), f32[1536,1024]{1,0:T(8,128)}) %reduce-scatter.17.cloned.1.call-update) | async-done | bytes 6291472 | tf_op jit(solution)/shard_map/reduce_scatter | solution.py:92
  1063.5 9.9 fusion.37
  1074.1 79.9 %all-gather.20.cloned.1.call-done = bf16[3072,1024]{1,0:T(8,128)(2,1)} async-done(((bf16[1536,1024]{1,0:T(8,128)(2,1)}), bf16[3072,1024]{1,0:T(8,128)(2,1)}) %all-gather.20.cloned.1.call-update) | async-done | bytes 6291472 | tf_op jit(solution)/shard_map/all_gather | solution.py:99
  1154.0 10.0 fusion.69
  1164.1 72.4 %all-gather.22.cloned.1.call-done = bf16[3072,1024]{1,0:T(8,128)(2,1)} async-done(((bf16[1536,1024]{1,0:T(8,128)(2,1)}), bf16[3072,1024]{1,0:T(8,128)(2,1)}) %all-gather.22.cloned.1.call-update) | async-done | bytes 6291472 | tf_op jit(solution)/shard_map/all_gather | solution.py:100
  1236.5 10.6 add_convert_fusion.1
  1247.1 85.4 %reduce-scatter.25.cloned.1.call-done = bf16[768,768]{1,0:T(8,128)(2,1)} async-done(((bf16[3072,768]{1,0:T(8,128)(2,1)}), bf16[768,768]{1,0:T(8,128)(2,1)}) %reduce-scatter.25.cloned.1.call-update) | async-done | bytes 1179664 | tf_op jit(solution)/shard_map/reduce_scatter | solution.py:75
  1344.7 90.0 %all-gather.24.cloned.1.call-done = bf16[3072,768]{1,0:T(8,128)(2,1)} async-done(((bf16[768,768]{1,0:T(8,128)(2,1)}), bf16[3072,768]{1,0:T(8,128)(2,1)}) %all-gather.24.cloned.1.call-update) | async-done | bytes 4718608 | tf_op jit(solution)/shard_map/all_gather | solution.py:71
  1434.8 6.5 convolution_convert_fusion.3
  1442.1 32.5 %reduce-scatter.27.cloned.1.call-done = bf16[1536,384]{1,0:T(8,128)(2,1)} async-done(((bf16[3072,384]{1,0:T(8,128)(2,1)}), bf16[1536,384]{1,0:T(8,128)(2,1)}) %reduce-scatter.27.cloned.1.call-update) | async-done | bytes 1179664 | tf_op jit(solution)/shard_map/reduce_scatter | solution.py:85
  1477.0 203.3 %while.32 = (s32[]{:T(128)}, f32[1536,6,64]{0,2,1:T(8,128)}, f32[1536,6,64]{0,2,1:T(8,128)}, f32[6,1536]{1,0:T(8,128)S(1)}, bf16[3,512,6,64]{1,3,2,0:T(8,128)(2,...) while((s32[]{:T(128)}, f32[1536,6,64]{0,2,1:T(8,128)}, ...), condition=%wide.region_33.34_spmd.clone, body=%wide.region_29.33_spmd.clone.sunk | while | flops 3093238784 | bytes 276796800 | solution.py:236
  1481.9 10.7 fusion.149
  1492.7 15.2 multiply_reduce_fusion.3
  1507.9 16.3 convert_reduce_fusion.4
  1532.8 7.8 fusion.153
  1549.7 9.2 fusion.149
  1558.8 15.2 multiply_reduce_fusion.3
  1574.0 16.3 convert_reduce_fusion.4
  1594.6 5.2 fusion.152
  1599.8 7.8 fusion.153
  1617.5 9.2 fusion.149
  1626.6 15.2 multiply_reduce_fusion.3
  1641.8 16.3 convert_reduce_fusion.4
  1667.6 7.8 fusion.153
  1691.1 9.6 convolution_convert_fusion.6
  1700.7 10.4 convolution_convert_fusion.7
  1711.1 9.6 convolution_convert_fusion.5
  1726.5 7.4 reduce-window.36
  1734.3 46.6 %all-gather.26.cloned.1.call-done = bf16[3072,1152]{0,1:T(8,128)(2,1)} async-done(((bf16[1536,1152]{0,1:T(8,128)(2,1)}), bf16[3072,1152]{0,1:T(8,128)(2,1)}) %all-gather.26.cloned.1.call-update) | async-done | bytes 7077904 | tf_op jit(solution)/shard_map/all_gather | solution.py:99
  1780.9 11.2 convolution_convert_fusion.4
  1792.2 7.7 reduce-window.34
  1805.0 8.8 fusion.70
  1818.7 9.5 convolution_convert_fusion.1
  1831.5 12.0 all-reduce.4
  1844.6 81.0 %all-reduce.8.cloned.1.call-done = (bf16[768,1152]{1,0:T(8,128)(2,1)}, bf16[384,768]{1,0:T(8,128)(2,1)}, bf16[768,1024]{1,0:T(8,128)(2,1)}, bf16[768,1024]{1,0:T(8,128)(2,1)}, bf16[1024,768]{1,0:T(8,128)(2,1)}) async-done(((bf16[768,1152]{1,0:T(8,128)(2,1)}, bf16[384,768]{1,0:T(8,128)(2,1)}, bf16[768,1024]{1,0:T(8,128)(2,1)}, bf16[768,1024]{1,0:T(8,128)(2,1)}, bf16[1024,768]{1,0:T(8,128)(2,1)}), ...) | async-done | bytes 7077904 | tf_op jit(solution)/shard_map/psum | solution.py:268
  1935.9 77.4 %reduce-scatter.29.cloned.1.call-done = bf16[768,768]{1,0:T(8,128)(2,1)} async-done(((bf16[3072,768]{1,0:T(8,128)(2,1)}), bf16[768,768]{1,0:T(8,128)(2,1)}) %reduce-scatter.29.cloned.1.call-update) | async-done | bytes 1179664 | tf_op jit(solution)/shard_map/reduce_scatter | solution.py:75
  2015.7 36.5 %all-reduce.3 = (f32[768]{0:T(1024)}, f32[768]{0:T(1024)}) all-reduce(f32[768]{0:T(1024)S(1)} %get-tuple-element.219, f32[768]{0:T(1024)S(1)} %copy-done.35), channel_id=1, replica_groups=mesh['dp'=4,'row'=2,'col'=4] {'dp','col'}, use_global_device_ids=true, to_apply=%region_46.47 | all-reduce | flops 1536 | bytes 12288 | tf_op jit(solution)/shard_map/psum | solution.py:266
  2057.1 46.4 %reduce-scatter.21.cloned.1.call-done = bf16[768,768]{1,0:T(8,128)(2,1)} async-done(((bf16[3072,768]{1,0:T(8,128)(2,1)}), bf16[768,768]{1,0:T(8,128)(2,1)}) %reduce-scatter.21.cloned.1.call-update) | async-done | bytes 1179664 | tf_op jit(solution)/shard_map/reduce_scatter | solution.py:75
  (311 shorter events, 154.5 us)
Async XLA Ops:
  7.2 107.2 %copy-start = (bf16[768,1152]{1,0:T(8,128)(2,1)S(1)}, bf16[768,1152]{1,0:T(8,128)(2,1)}, u32[]{:S(2)}) copy-start(bf16[768,1152]{1,0:T(8,128)(2,1)} %param.20) | copy-start | bytes 5308420
  7.2 102.8 %copy-start.20 = (bf16[768,6]{0,1:T(8,128)(2,1)S(1)}, bf16[768,6]{0,1:T(8,128)(2,1)}, u32[]{:S(2)}) copy-start(bf16[768,6]{0,1:T(8,128)(2,1)} %param.21) | copy-start | bytes 27652
  7.2 102.8 %all-gather.10.cloned.1.call-start = ((), (), s32[]{:S(2)}) async-start(), calls=%async_computation.10 | async-start | bytes 5898240 | tf_op jit(solution)/shard_map/all_gather | solution.py:71
  18.6 108.0 %reduce-scatter.13.cloned.1.call-start = ((), (), s32[]{:S(2)}) async-start(), calls=%async_computation.12 | async-start | bytes 147456 | tf_op jit(solution)/shard_map/reduce_scatter | solution.py:93
  114.3 172.5 %reduce-scatter.11.cloned.1.call-start = ((), (), s32[]{:S(2)}) async-start(), calls=%async_computation.11 | async-start | bytes 21233664 | tf_op jit(solution)/shard_map/reduce_scatter | solution.py:92
  125.5 293.2 %all-gather.12.cloned.1.call-start = ((), (), s32[]{:S(2)}) async-start(), calls=%async_computation.13 | async-start | bytes 3538944 | tf_op jit(solution)/shard_map/all_gather | solution.py:81
  126.5 165.5 %copy-start.39 = (pred[4,4]{1,0:T(4,128)(4,1)}, pred[4,4]{1,0:T(4,128)(4,1)S(1)}, u32[]{:S(2)}) copy-start(pred[4,4]{1,0:T(4,128)(4,1)S(1)} %iota_compare_fusion.6) | copy-start | bytes 52
  126.5 3.7 copy-start.30
  126.5 6.0 copy-start.32
  126.6 3.6 copy-start.23
  304.6 7.3 copy-start.3
  330.2 7.3 copy-start.3
  355.8 7.3 copy-start.3
  381.1 37.6 %copy-start.44 = (bf16[384,768]{1,0:T(8,128)(2,1)S(1)}, bf16[384,768]{1,0:T(8,128)(2,1)}, u32[]{:S(2)}) copy-start(bf16[384,768]{1,0:T(8,128)(2,1)} %param.23) | copy-start | bytes 1769476
  382.5 128.1 %reduce-scatter.15.cloned.1.call-start = ((), (), s32[]{:S(2)}) async-start(), calls=%async_computation.14 | async-start | bytes 5898240 | tf_op jit(solution)/shard_map/reduce_scatter | solution.py:75
  425.2 85.5 %copy-start.4 = (bf16[768,768]{1,0:T(8,128)(2,1)S(1)}, bf16[768,768]{1,0:T(8,128)(2,1)}, u32[]{:S(2)}) copy-start(bf16[768,768]{1,0:T(8,128)(2,1)} %param.18) | copy-start | bytes 3538948
  425.2 92.1 %copy-start.18 = (f32[768]{0:T(1024)S(1)}, f32[768]{0:T(1024)}, u32[]{:S(2)}) copy-start(f32[768]{0:T(1024)} %param.24) | copy-start | bytes 9220
  425.2 176.8 %all-gather.18.cloned.1.call-start = ((), (), s32[]{:S(2)}) async-start(), calls=%async_computation.20 | async-start | bytes 5898240 | tf_op jit(solution)/shard_map/all_gather | solution.py:71
  425.8 266.3 %all-gather.14.cloned.1.call-start = ((), (), s32[]{:S(2)}) async-start(), calls=%async_computation.15 | async-start | bytes 5898240 | tf_op jit(solution)/shard_map/all_gather | solution.py:71
  517.3 823.4 %copy-start.14 = (f32[768]{0:T(1024)}, f32[768]{0:T(1024)S(1)}, u32[]{:S(2)}) copy-start(f32[768]{0:T(1024)S(1)} %get-tuple-element.300) | copy-start | bytes 9220
  517.3 823.4 %copy-start.25 = (f32[768]{0:T(1024)}, f32[768]{0:T(1024)S(1)}, u32[]{:S(2)}) copy-start(f32[768]{0:T(1024)S(1)} %get-tuple-element.299) | copy-start | bytes 9220
  520.1 249.8 %reduce-scatter.23.cloned.1.call-start = ((), (), s32[]{:S(2)}) async-start(), calls=%async_computation.21 | async-start | bytes 9437184 | tf_op jit(solution)/shard_map/reduce_scatter | solution.py:85
  611.7 305.1 %reduce-scatter.19.cloned.1.call-start = ((), (), s32[]{:S(2)}) async-start(), calls=%async_computation.17 | async-start | bytes 18874368 | tf_op jit(solution)/shard_map/reduce_scatter | solution.py:93
  702.1 361.5 %reduce-scatter.17.cloned.1.call-start = ((), (), s32[]{:S(2)}) async-start(), calls=%async_computation.16 | async-start | bytes 18874368 | tf_op jit(solution)/shard_map/reduce_scatter | solution.py:92
  712.6 441.4 %all-gather.20.cloned.1.call-start = ((), (), s32[]{:S(2)}) async-start(), calls=%async_computation.22 | async-start | bytes 9437184 | tf_op jit(solution)/shard_map/all_gather | solution.py:99
  1073.5 163.0 %all-gather.22.cloned.1.call-start = ((), (), s32[]{:S(2)}) async-start(), calls=%async_computation.23 | async-start | bytes 9437184 | tf_op jit(solution)/shard_map/all_gather | solution.py:100
  1074.1 258.4 %reduce-scatter.25.cloned.1.call-start = ((), (), s32[]{:S(2)}) async-start(), calls=%async_computation.24 | async-start | bytes 5898240 | tf_op jit(solution)/shard_map/reduce_scatter | solution.py:75
  1247.1 187.7 %all-gather.24.cloned.1.call-start = ((), (), s32[]{:S(2)}) async-start(), calls=%async_computation.25 | async-start | bytes 5898240 | tf_op jit(solution)/shard_map/all_gather | solution.py:71
  1340.7 4.0 copy-start.27
  1344.7 130.0 %reduce-scatter.27.cloned.1.call-start = ((), (), s32[]{:S(2)}) async-start(), calls=%async_computation.26 | async-start | bytes 3538944 | tf_op jit(solution)/shard_map/reduce_scatter | solution.py:85
  1441.3 269.8 %all-gather.16.cloned.1.call-start = ((), (), s32[]{:S(2)}) async-start(), calls=%async_computation.18 | async-start | bytes 9437184 | tf_op jit(solution)/shard_map/all_gather | solution.py:81
  1441.4 35.6 %copy-start.6 = (bf16[1536,6,64]{0,2,1:T(8,128)(2,1)S(1)}, bf16[1536,6,64]{0,2,1:T(8,128)(2,1)}, u32[]{:S(2)}) copy-start(bf16[1536,6,64]{0,2,1:T(8,128)(2,1)} %get-tuple-element.600) | copy-start | bytes 3538948
  1441.9 338.9 %all-gather.26.cloned.1.call-start = ((), (), s32[]{:S(2)}) async-start(), calls=%async_computation.27 | async-start | bytes 10616832 | tf_op jit(solution)/shard_map/all_gather | solution.py:99
  1481.9 10.8 copy-start.12
  1507.9 20.6 copy-start.1
  1532.8 7.8 copy-start.2
  1549.7 9.2 copy-start.12
  1574.0 20.6 copy-start.1
  1599.8 7.8 copy-start.2
  1617.5 9.2 copy-start.12
  1641.8 20.6 copy-start.1
  1667.6 7.8 copy-start.2
  1685.7 2.9 copy-start.7
  1691.1 234.5 %all-reduce.8.cloned.1.call-start = ((), (), s32[]{:S(2)}) async-start(), calls=%async_computation.29 | async-start | bytes 14155776 | tf_op jit(solution)/shard_map/psum | solution.py:268
  1711.1 9.7 copy-start.42
  1720.7 5.2 copy-start.33
  1720.7 5.4 copy-start.40
  1720.8 5.6 copy-start.24
  1792.0 8.2 copy-start.31
  1792.0 8.4 copy-start.13
  1792.0 8.4 copy-start.38
  1792.0 221.3 %reduce-scatter.29.cloned.1.call-start = ((), (), s32[]{:S(2)}) async-start(), calls=%async_computation.28 | async-start | bytes 5898240 | tf_op jit(solution)/shard_map/reduce_scatter | solution.py:75
  1805.0 8.8 copy-start.21
  1817.4 286.2 %reduce-scatter.21.cloned.1.call-start = ((), (), s32[]{:S(2)}) async-start(), calls=%async_computation.19 | async-start | bytes 5898240 | tf_op jit(solution)/shard_map/reduce_scatter | solution.py:75
  1925.6 2.3 copy-start.8
  1934.0 79.3 %copy-start.5 = (bf16[768,768]{1,0:T(8,128)(2,1)S(1)}, bf16[768,768]{1,0:T(8,128)(2,1)}, u32[]{:S(2)}) copy-start(bf16[768,768]{1,0:T(8,128)(2,1)} %param.18) | copy-start | bytes 3538948
  1934.0 79.3 %copy-start.17 = (f32[768]{0:T(1024)S(1)}, f32[768]{0:T(1024)}, u32[]{:S(2)}) copy-start(f32[768]{0:T(1024)} %copy-done.16) | copy-start | bytes 9220
  1934.0 79.3 %copy-start.22 = (f32[768]{0:T(1024)S(1)}, f32[768]{0:T(1024)}, u32[]{:S(2)}) copy-start(f32[768]{0:T(1024)} %param.19) | copy-start | bytes 9220
  1935.9 79.8 %copy-start.35 = (f32[768]{0:T(1024)S(1)}, f32[768]{0:T(1024)}, u32[]{:S(2)}) copy-start(f32[768]{0:T(1024)} %get-tuple-element.217) | copy-start | bytes 9220
  1935.9 167.6 %copy-start.15 = (f32[768]{0:T(1024)S(1)}, f32[768]{0:T(1024)}, u32[]{:S(2)}) copy-start(f32[768]{0:T(1024)} %copy-done.14) | copy-start | bytes 9220
  1935.9 167.6 %copy-start.19 = (f32[768]{0:T(1024)S(1)}, f32[768]{0:T(1024)}, u32[]{:S(2)}) copy-start(f32[768]{0:T(1024)} %param.24) | copy-start | bytes 9220
  1935.9 167.6 %copy-start.26 = (f32[768]{0:T(1024)S(1)}, f32[768]{0:T(1024)}, u32[]{:S(2)}) copy-start(f32[768]{0:T(1024)} %copy-done.25) | copy-start | bytes 9220
  1935.9 167.6 %copy-start.28 = (f32[768]{0:T(1024)S(1)}, f32[768]{0:T(1024)}, u32[]{:S(2)}) copy-start(f32[768]{0:T(1024)} %copy-done.27) | copy-start | bytes 9220
  1935.9 167.6 %copy-start.34 = (f32[768]{0:T(1024)S(1)}, f32[768]{0:T(1024)}, u32[]{:S(2)}) copy-start(f32[768]{0:T(1024)} %get-tuple-element.297) | copy-start | bytes 9220
  (9 other events, 11.4 us)
Sparse Core Ops, SparseCore 0:
  18.7 91.2 all-gather.9
  114.4 8.4 reduce-scatter.12
  125.6 161.1 reduce-scatter.10
  382.6 36.0 all-gather.11
  425.3 85.2 reduce-scatter.14
  512.0 89.9 all-gather.17
  604.1 87.8 all-gather.13
  694.3 75.5 reduce-scatter.22
  772.3 144.4 reduce-scatter.18
  919.1 144.4 reduce-scatter.16
  1073.6 80.3 all-gather.19
  1156.1 80.3 all-gather.21
  1247.2 85.2 reduce-scatter.24
  1344.8 89.9 all-gather.23
  1441.5 33.1 reduce-scatter.26
  1476.6 80.3 all-gather.15
  1691.2 89.5 all-gather.25
  1792.2 133.3 all-reduce.7
  1927.9 85.4 reduce-scatter.28
  2015.5 87.9 reduce-scatter.20
where the time goes:
time: 2120 us
  waiting for transfers between devices  1490 us (70%)
  matrix products  325 us (15%)
  other arithmetic  153 us (7%)
  blocking collectives  73.6 us (3%)
  local copies, waits for them, and re-layouts  44.4 us (2%)
    all_gather x4, waiting for transfers between devices, gather_tokens(): return lax.all_gather(token_rows, 'col', axis=0, tiled=True)  344 us
    reduce_scatter x2, waiting for transfers between devices, sum_pair(): lax.psum_scatter(first, 'row', scatter_dimension=0, tiled=True)  301 us
    reduce_scatter x4, waiting for transfers between devices, sum_tokens(): lax.psum_scatter(partial_value.astype(jnp.bfloat16), 'col', scatter_dimen...  294 us
    reduce_scatter x2, waiting for transfers between devices, sum_pair(): lax.psum_scatter(second, 'row', scatter_dimension=0, tiled=True)  147 us
    all_gather x2, waiting for transfers between devices, gather_pair(): lax.all_gather(first, 'row', axis=0, tiled=True)  127 us
    reduce_scatter x2, waiting for transfers between devices, sum_group(): lax.psum_scatter(partial_value.astype(jnp.bfloat16), 'row', scatter_dimen...  89.7 us
    psum x1, waiting for transfers between devices, shards(): lax.psum(qkv_grad.astype(jnp.bfloat16), 'dp').astype(jnp.float32)  81 us
    all_gather x1, waiting for transfers between devices, gather_pair(): lax.all_gather(second, 'row', axis=0, tiled=True)  72.4 us
  transfers between devices with their start and end apart: 20, of which 18 were waited for; matrix products, arithmetic and copies ran while one was open for 16% of the time, Pallas kernels for 0%

commit v1 on v0

--- a/solution.py
+++ b/solution.py
@@ -1,7 +1,9 @@
+import functools
 import jax
 import jax.numpy as jnp
 from jax import lax
 from jax.sharding import PartitionSpec as P
+from jax.lax import axis_index, axis_size, ppermute
 
 D = 1536
 DH = 64
@@ -9,6 +11,29 @@
 QBLK = 512
 EPS = 1e-06
 MASKED = -1e30
+
+
+def load_the_results(own_rows, peer_axis):
+    piece_out, t1, even = (axis_size(peer_axis), axis_index(peer_axis), own_rows.shape[0])
+    slots = [i0 * piece_out if it == 0 else i0 for it, i0 in enumerate(own_rows.shape)]
+    aux = lax.dynamic_update_slice_in_dim(
+        jnp.zeros(slots, own_rows.dtype), own_rows, t1 * even, axis=0
+    )
+    seen_now = o_now = own_rows
+    for u in [*range(1, piece_out // 2 + 1)]:
+        seen_now = ppermute(
+            seen_now, peer_axis, [(it, (it + 1) % piece_out) for it in range(piece_out)]
+        )
+        aux = lax.dynamic_update_slice_in_dim(aux, seen_now, (t1 - u) % piece_out * even, axis=0)
+        if 2 * u < piece_out:
+            o_now = ppermute(
+                o_now, peer_axis, [(it, (it - 1) % piece_out) for it in range(piece_out)]
+            )
+            aux = lax.dynamic_update_slice_in_dim(aux, o_now, (t1 + u) % piece_out * even, axis=0)
+    return aux
+
+
+tables_fit = functools.partial(load_the_results, peer_axis="col")
 
 
 def visible(row_start, doc_query, branch_query, doc_key, branch_key):
@@ -68,7 +93,7 @@
 
 
 def gather_tokens(token_rows):
-    return lax.all_gather(token_rows, "col", axis=0, tiled=True)
+    return tables_fit(token_rows)
 
 
 def sum_tokens(partial_value):

time: 2120 us -> 2010 us (0.948)
  waiting for transfers between devices: 1490 us -> 1270 us
  starting transfers between devices: 1 us -> 110 us
  local copies, waits for them, and re-layouts: 44.4 us -> 65.8 us
    all_gather x4 -> x0, waiting for transfers between devices: 344 us -> none  [gather_tokens(): return lax.all_gather(token_rows, 'col', axis=0, tiled=True)]
    ppermute x0 -> x12, waiting for transfers between devices: none -> 273 us  [the longest x8 241 us: load_the_results(): ppermute(seen_now, peer_axis, [(it, (it + 1) % piece_out) for it in range...]
    ppermute x0 -> x12, starting transfers between devices: none -> 110 us  [the longest x8 99.7 us: load_the_results(): ppermute(seen_now, peer_axis, [(it, (it + 1) % piece_out) for it in range...]
    reduce_scatter x4, waiting for transfers between devices: 294 us -> 207 us  [sum_tokens(): lax.psum_scatter(partial_value.astype(jnp.bfloat16), 'col', scatter_dimen...]
    reduce_scatter x2, waiting for transfers between devices: 89.7 us -> 32.9 us  [sum_group(): lax.psum_scatter(partial_value.astype(jnp.bfloat16), 'row', scatter_dimen...]
  transfers between devices with their start and end apart: 20 -> 28, of which waited for: 18 -> 24; matrix products, arithmetic and copies ran while one was open for 16% -> 17% of each run, Pallas kernels for 0% -> 0%
where the time goes in v1:
time: 2010 us
  waiting for transfers between devices  1270 us (63%)
  matrix products  318 us (16%)
  other arithmetic  148 us (7%)
  starting transfers between devices  110 us (5%)
  blocking collectives  73.6 us (4%)
  local copies, waits for them, and re-layouts  65.8 us (3%)
    reduce_scatter x2, waiting for transfers between devices, sum_pair(): lax.psum_scatter(first, 'row', scatter_dimension=0, tiled=True)  302 us
    ppermute x8, waiting for transfers between devices, load_the_results(): ppermute(seen_now, peer_axis, [(it, (it + 1) % piece_out) for it in range...  241 us
    reduce_scatter x4, waiting for transfers between devices, sum_tokens(): lax.psum_scatter(partial_value.astype(jnp.bfloat16), 'col', scatter_dimen...  207 us
    reduce_scatter x2, waiting for transfers between devices, sum_pair(): lax.psum_scatter(second, 'row', scatter_dimension=0, tiled=True)  132 us
    all_gather x2, waiting for transfers between devices, gather_pair(): lax.all_gather(first, 'row', axis=0, tiled=True)  126 us
    ppermute x8, starting transfers between devices, load_the_results(): ppermute(seen_now, peer_axis, [(it, (it + 1) % piece_out) for it in range...  99.7 us
    psum x1, waiting for transfers between devices, shards(): lax.psum(qkv_grad.astype(jnp.bfloat16), 'dp').astype(jnp.float32)  81 us
    all_gather x1, waiting for transfers between devices, gather_pair(): lax.all_gather(second, 'row', axis=0, tiled=True)  72.6 us
  transfers between devices with their start and end apart: 28, of which 24 were waited for; matrix products, arithmetic and copies ran while one was open for 17% of the time, Pallas kernels for 0%

profile of v1, /device:TPU:0, one launch (start us, length us, event | category | flops | bytes accessed | tf_op | source)
XLA Modules:
  0.0 2006.2 jit_solution(18038580967893550883)
XLA Ops:
  23.5 27.1 %collective-permute-done = bf16[768,768]{1,0:T(8,128)(2,1)S(1)} collective-permute-done((bf16[768,768]{1,0:T(8,128)(2,1)}, bf16[768,768]{1,0:T(8,128)(2,1)S(1)}, u32[]{:S(2)}, u32[]{:S(2)}) %collective-permute-start) | collective-permute-done | bytes 1179680 | tf_op jit(solution)/shard_map/ppermute | solution.py:24
  50.6 21.2 %collective-permute-start.2 = (bf16[768,768]{1,0:T(8,128)(2,1)S(1)}, bf16[768,768]{1,0:T(8,128)(2,1)}, u32[]{:S(2)}, u32[]{:S(2)}) collective-permute-start(bf16[768,768]{1,0:T(8,128)(2,1)S(1)} %collective-permute-done), channel_id=1, source_target_pairs={{0,1},{1,2},{2,3},{3,0},{4,5},{5,6},{6,7},{7,4},{8,9},{9,10},{10,1... | collective-permute-start | bytes 3538952 | tf_op jit(solution)/shard_map/ppermute | solution.py:24
  77.1 22.1 %collective-permute-done.2 = bf16[768,768]{1,0:T(8,128)(2,1)} collective-permute-done((bf16[768,768]{1,0:T(8,128)(2,1)S(1)}, bf16[768,768]{1,0:T(8,128)(2,1)}, u32[]{:S(2)}, u32[]{:S(2)}) %collective-permute-start.2) | collective-permute-done | bytes 1179680 | tf_op jit(solution)/shard_map/ppermute | solution.py:24
  105.9 11.1 fusion.67
  124.2 155.0 %reduce-scatter.11.cloned.1.call-done = f32[1536,1152]{1,0:T(8,128)} async-done(((f32[3072,1152]{1,0:T(8,128)}), f32[1536,1152]{1,0:T(8,128)}) %reduce-scatter.11.cloned.1.call-update) | async-done | bytes 7077904 | tf_op jit(solution)/shard_map/reduce_scatter | solution.py:117
  294.0 77.2 %while.31 = (s32[]{:T(128)}, bf16[3,512,6,64]{1,3,2,0:T(8,128)(2,1)}, f32[3,6,512]{2,1,0:T(8,128)S(1)}, s32[3]{0:T(128)S(1)}, s32[1536]{0:T(1024)S(1)}, /*index=...) while((s32[]{:T(128)}, ...), condition=%wide.region_17.18_spmd, body=%wide.region_14.17_spmd.sunk | while | flops 1297808384 | bytes 66381052 | solution.py:189
  297.0 7.2 fusion.139
  304.3 6.5 fusion.140
  310.8 8.9 fusion.141
  322.6 7.2 fusion.139
  329.9 6.5 fusion.140
  336.4 8.9 fusion.141
  348.2 7.2 fusion.139
  362.0 8.9 fusion.141
  374.9 36.2 %all-gather.6.cloned.1.call-done = bf16[3072,384]{0,1:T(8,128)(2,1)} async-done(((bf16[1536,384]{0,1:T(8,128)(2,1)}), bf16[3072,384]{0,1:T(8,128)(2,1)}) %all-gather.6.cloned.1.call-update) | async-done | bytes 2359312 | tf_op jit(solution)/shard_map/all_gather | solution.py:106
  422.7 48.7 %collective-permute-done.6 = bf16[768,768]{1,0:T(8,128)(2,1)S(1)} collective-permute-done((bf16[768,768]{1,0:T(8,128)(2,1)S(1)}, bf16[768,768]{1,0:T(8,128)(2,1)S(1)}, u32[]{:S(2)}, u32[]{:S(2)}) %collective-permute-start.6) | collective-permute-done | bytes 1179680 | tf_op jit(solution)/shard_map/ppermute | solution.py:24
  471.4 31.0 %collective-permute-start.8 = (bf16[768,768]{1,0:T(8,128)(2,1)S(1)}, bf16[768,768]{1,0:T(8,128)(2,1)S(1)}, u32[]{:S(2)}, u32[]{:S(2)}) collective-permute-start(bf16[768,768]{1,0:T(8,128)(2,1)S(1)} %collective-permute-done.6), channel_id=1, source_target_pairs={{0,1},{1,2},{2,3},{3,0},{4,5},{5,6},{6,7},{7,4},{8,9},{9,10},{10,1... | collective-permute-start | bytes 3538952 | tf_op jit(solution)/shard_map/ppermute | solution.py:24
  502.9 24.6 %collective-permute-done.7 = bf16[768,768]{1,0:T(8,128)(2,1)S(1)} collective-permute-done((bf16[768,768]{1,0:T(8,128)(2,1)S(1)}, bf16[768,768]{1,0:T(8,128)(2,1)S(1)}, u32[]{:S(2)}, u32[]{:S(2)}) %collective-permute-start.7) | collective-permute-done | bytes 1179680 | tf_op jit(solution)/shard_map/ppermute | solution.py:29
  527.6 43.8 %collective-permute-done.8 = bf16[768,768]{1,0:T(8,128)(2,1)S(1)} collective-permute-done((bf16[768,768]{1,0:T(8,128)(2,1)S(1)}, bf16[768,768]{1,0:T(8,128)(2,1)S(1)}, u32[]{:S(2)}, u32[]{:S(2)}) %collective-permute-start.8) | collective-permute-done | bytes 1179680 | tf_op jit(solution)/shard_map/ppermute | solution.py:24
  573.7 7.4 convolution_convert_fusion
  594.7 26.9 %collective-permute-done.3 = bf16[768,768]{1,0:T(8,128)(2,1)S(1)} collective-permute-done((bf16[768,768]{1,0:T(8,128)(2,1)S(1)}, bf16[768,768]{1,0:T(8,128)(2,1)S(1)}, u32[]{:S(2)}, u32[]{:S(2)}) %collective-permute-start.3) | collective-permute-done | bytes 1179680 | tf_op jit(solution)/shard_map/ppermute | solution.py:24
  621.5 20.1 %collective-permute-start.5 = (bf16[768,768]{1,0:T(8,128)(2,1)S(1)}, bf16[768,768]{1,0:T(8,128)(2,1)S(1)}, u32[]{:S(2)}, u32[]{:S(2)}) collective-permute-start(bf16[768,768]{1,0:T(8,128)(2,1)S(1)} %collective-permute-done.3), channel_id=1, source_target_pairs={{0,1},{1,2},{2,3},{3,0},{4,5},{5,6},{6,7},{7,4},{8,9},{9,10},{10,1... | collective-permute-start | bytes 3538952 | tf_op jit(solution)/shard_map/ppermute | solution.py:24
  645.3 21.4 %collective-permute-done.5 = bf16[768,768]{1,0:T(8,128)(2,1)S(1)} collective-permute-done((bf16[768,768]{1,0:T(8,128)(2,1)S(1)}, bf16[768,768]{1,0:T(8,128)(2,1)S(1)}, u32[]{:S(2)}, u32[]{:S(2)}) %collective-permute-start.5) | collective-permute-done | bytes 1179680 | tf_op jit(solution)/shard_map/ppermute | solution.py:24
  668.8 8.0 fusion.70
  676.9 10.4 fusion.69
  687.5 132.4 %reduce-scatter.19.cloned.1.call-done = f32[1536,1024]{1,0:T(8,128)} async-done(((f32[3072,1024]{1,0:T(8,128)}), f32[1536,1024]{1,0:T(8,128)}) %reduce-scatter.19.cloned.1.call-update) | async-done | bytes 6291472 | tf_op jit(solution)/shard_map/reduce_scatter | solution.py:118
  819.9 146.9 %reduce-scatter.17.cloned.1.call-done = f32[1536,1024]{1,0:T(8,128)} async-done(((f32[3072,1024]{1,0:T(8,128)}), f32[1536,1024]{1,0:T(8,128)}) %reduce-scatter.17.cloned.1.call-update) | async-done | bytes 6291472 | tf_op jit(solution)/shard_map/reduce_scatter | solution.py:117
  966.8 9.9 fusion.37
  977.5 79.8 %all-gather.10.cloned.1.call-done = bf16[3072,1024]{1,0:T(8,128)(2,1)} async-done(((bf16[1536,1024]{1,0:T(8,128)(2,1)}), bf16[3072,1024]{1,0:T(8,128)(2,1)}) %all-gather.10.cloned.1.call-update) | async-done | bytes 6291472 | tf_op jit(solution)/shard_map/all_gather | solution.py:124
  1057.3 10.0 fusion.71
  1067.3 72.6 %all-gather.12.cloned.1.call-done = bf16[3072,1024]{1,0:T(8,128)(2,1)} async-done(((bf16[1536,1024]{1,0:T(8,128)(2,1)}), bf16[3072,1024]{1,0:T(8,128)(2,1)}) %all-gather.12.cloned.1.call-update) | async-done | bytes 6291472 | tf_op jit(solution)/shard_map/all_gather | solution.py:125
  1139.9 10.5 add_convert_fusion.1
  1150.5 85.4 %reduce-scatter.25.cloned.1.call-done = bf16[768,768]{1,0:T(8,128)(2,1)} async-done(((bf16[3072,768]{1,0:T(8,128)(2,1)}), bf16[768,768]{1,0:T(8,128)(2,1)}) %reduce-scatter.25.cloned.1.call-update) | async-done | bytes 1179664 | tf_op jit(solution)/shard_map/reduce_scatter | solution.py:100
  1251.1 26.9 %collective-permute-done.9 = bf16[768,768]{1,0:T(8,128)(2,1)S(1)} collective-permute-done((bf16[768,768]{1,0:T(8,128)(2,1)S(1)}, bf16[768,768]{1,0:T(8,128)(2,1)S(1)}, u32[]{:S(2)}, u32[]{:S(2)}) %collective-permute-start.9) | collective-permute-done | bytes 1179680 | tf_op jit(solution)/shard_map/ppermute | solution.py:24
  1278.0 21.6 %collective-permute-start.11 = (bf16[768,768]{1,0:T(8,128)(2,1)S(1)}, bf16[768,768]{1,0:T(8,128)(2,1)S(1)}, u32[]{:S(2)}, u32[]{:S(2)}) collective-permute-start(bf16[768,768]{1,0:T(8,128)(2,1)S(1)} %collective-permute-done.9), channel_id=1, source_target_pairs={{0,1},{1,2},{2,3},{3,0},{4,5},{5,6},{6,7},{7,4},{8,9},{9,10},{10,1... | collective-permute-start | bytes 3538952 | tf_op jit(solution)/shard_map/ppermute | solution.py:24
  1302.6 23.6 %collective-permute-done.11 = bf16[768,768]{1,0:T(8,128)(2,1)S(1)} collective-permute-done((bf16[768,768]{1,0:T(8,128)(2,1)S(1)}, bf16[768,768]{1,0:T(8,128)(2,1)S(1)}, u32[]{:S(2)}, u32[]{:S(2)}) %collective-permute-start.11) | collective-permute-done | bytes 1179680 | tf_op jit(solution)/shard_map/ppermute | solution.py:24
  1333.1 32.9 %reduce-scatter.27.cloned.1.call-done = bf16[1536,384]{1,0:T(8,128)(2,1)} async-done(((bf16[3072,384]{1,0:T(8,128)(2,1)}), bf16[1536,384]{1,0:T(8,128)(2,1)}) %reduce-scatter.27.cloned.1.call-update) | async-done | bytes 1179664 | tf_op jit(solution)/shard_map/reduce_scatter | solution.py:110
  1368.3 203.4 %while.32 = (s32[]{:T(128)}, f32[1536,6,64]{0,2,1:T(8,128)}, f32[1536,6,64]{0,2,1:T(8,128)}, f32[6,1536]{1,0:T(8,128)S(1)}, bf16[3,512,6,64]{1,3,2,0:T(8,128)(2,...) while((s32[]{:T(128)}, f32[1536,6,64]{0,2,1:T(8,128)}, ...), condition=%wide.region_33.34_spmd.clone, body=%wide.region_29.33_spmd.clone.sunk | while | flops 3093238784 | bytes 276796800 | solution.py:261
  1373.2 10.8 fusion.151
  1384.0 15.2 multiply_reduce_fusion.3
  1399.2 16.3 convert_reduce_fusion.4
  1424.1 7.8 fusion.155
  1441.0 9.2 fusion.151
  1450.1 15.2 multiply_reduce_fusion.3
  1465.3 16.3 convert_reduce_fusion.4
  1491.1 7.8 fusion.155
  1508.8 9.2 fusion.151
  1517.9 15.2 multiply_reduce_fusion.3
  1533.1 16.3 convert_reduce_fusion.4
  1558.9 7.8 fusion.155
  1582.4 9.5 convolution_convert_fusion.6
  1591.9 10.4 convolution_convert_fusion.7
  1602.4 9.6 convolution_convert_fusion.5
  1617.8 7.4 reduce-window.36
  1625.5 46.6 %all-gather.14.cloned.1.call-done = bf16[3072,1152]{0,1:T(8,128)(2,1)} async-done(((bf16[1536,1152]{0,1:T(8,128)(2,1)}), bf16[3072,1152]{0,1:T(8,128)(2,1)}) %all-gather.14.cloned.1.call-update) | async-done | bytes 7077904 | tf_op jit(solution)/shard_map/all_gather | solution.py:124
  1672.1 11.2 convolution_convert_fusion.4
  1683.5 7.7 reduce-window.34
  1696.3 8.8 fusion.72
  1710.0 9.5 convolution_convert_fusion.1
  1722.7 12.0 all-reduce.4
  1735.8 81.0 %all-reduce.8.cloned.1.call-done = (bf16[768,1152]{1,0:T(8,128)(2,1)}, bf16[384,768]{1,0:T(8,128)(2,1)}, bf16[768,1024]{1,0:T(8,128)(2,1)}, bf16[768,1024]{1,0:T(8,128)(2,1)}, bf16[1024,768]{1,0:T(8,128)(2,1)}) async-done(((bf16[768,1152]{1,0:T(8,128)(2,1)}, bf16[384,768]{1,0:T(8,128)(2,1)}, bf16[768,1024]{1,0:T(8,128)(2,1)}, bf16[768,1024]{1,0:T(8,128)(2,1)}, bf16[1024,768]{1,0:T(8,128)(2,1)}), ...) | async-done | bytes 7077904 | tf_op jit(solution)/shard_map/psum | solution.py:293
  1829.0 75.5 %reduce-scatter.29.cloned.1.call-done = bf16[768,768]{1,0:T(8,128)(2,1)} async-done(((bf16[3072,768]{1,0:T(8,128)(2,1)}), bf16[768,768]{1,0:T(8,128)(2,1)}) %reduce-scatter.29.cloned.1.call-update) | async-done | bytes 1179664 | tf_op jit(solution)/shard_map/reduce_scatter | solution.py:100
  1906.9 36.5 %all-reduce.3 = (f32[768]{0:T(1024)}, f32[768]{0:T(1024)}) all-reduce(f32[768]{0:T(1024)S(1)} %get-tuple-element.219, f32[768]{0:T(1024)S(1)} %copy-done.45), channel_id=1, replica_groups=mesh['dp'=4,'row'=2,'col'=4] {'dp','col'}, use_global_device_ids=true, to_apply=%region_46.47 | all-reduce | flops 1536 | bytes 12288 | tf_op jit(solution)/shard_map/psum | solution.py:291
  1948.2 46.4 %reduce-scatter.21.cloned.1.call-done = bf16[768,768]{1,0:T(8,128)(2,1)} async-done(((bf16[3072,768]{1,0:T(8,128)(2,1)}), bf16[768,768]{1,0:T(8,128)(2,1)}) %reduce-scatter.21.cloned.1.call-update) | async-done | bytes 1179664 | tf_op jit(solution)/shard_map/reduce_scatter | solution.py:100
  (366 shorter events, 232.9 us)
Async XLA Ops:
  7.2 98.7 %copy-start = (bf16[768,1152]{1,0:T(8,128)(2,1)S(1)}, bf16[768,1152]{1,0:T(8,128)(2,1)}, u32[]{:S(2)}) copy-start(bf16[768,1152]{1,0:T(8,128)(2,1)} %param.20) | copy-start | bytes 5308420
  7.2 8.6 copy-start.4
  7.2 8.6 copy-start.37
  7.2 110.9 %reduce-scatter.13.cloned.1.call-start = ((), (), s32[]{:S(2)}) async-start(), calls=%async_computation.11 | async-start | bytes 147456 | tf_op jit(solution)/shard_map/reduce_scatter | solution.py:118
  19.3 31.3 %collective-permute-start = (bf16[768,768]{1,0:T(8,128)(2,1)}, bf16[768,768]{1,0:T(8,128)(2,1)S(1)}, u32[]{:S(2)}, u32[]{:S(2)}) collective-permute-start(bf16[768,768]{1,0:T(8,128)(2,1)} %get-tuple-element.286), channel_id=1, source_target_pairs={{0,1},{1,2},{2,3},{3,0},{4,5},{5,6},{6,7},{7,4},{8,9},{9,10},{10,1... | collective-permute-start | bytes 3538952 | tf_op jit(solution)/shard_map/ppermute | solution.py:24
  21.4 53.3 %collective-permute-start.1 = (bf16[768,768]{1,0:T(8,128)(2,1)}, bf16[768,768]{1,0:T(8,128)(2,1)}, u32[]{:S(2)}, u32[]{:S(2)}) collective-permute-start(bf16[768,768]{1,0:T(8,128)(2,1)} %get-tuple-element.286), channel_id=1, source_target_pairs={{0,3},{1,0},{2,1},{3,2},{4,7},{5,4},{6,5},{7,6},{8,11},{9,8},{10,9... | collective-permute-start | bytes 3538952 | tf_op jit(solution)/shard_map/ppermute | solution.py:29
  50.6 48.6 %collective-permute-start.2 = (bf16[768,768]{1,0:T(8,128)(2,1)S(1)}, bf16[768,768]{1,0:T(8,128)(2,1)}, u32[]{:S(2)}, u32[]{:S(2)}) collective-permute-start(bf16[768,768]{1,0:T(8,128)(2,1)S(1)} %collective-permute-done), channel_id=1, source_target_pairs={{0,1},{1,2},{2,3},{3,0},{4,5},{5,6},{6,7},{7,4},{8,9},{9,10},{10,1... | collective-permute-start | bytes 3538952 | tf_op jit(solution)/shard_map/ppermute | solution.py:24
  71.8 29.8 %copy-start.29 = (bf16[768,6]{0,1:T(8,128)(2,1)S(1)}, bf16[768,6]{0,1:T(8,128)(2,1)}, u32[]{:S(2)}) copy-start(bf16[768,6]{0,1:T(8,128)(2,1)} %param.21) | copy-start | bytes 27652
  105.9 173.3 %reduce-scatter.11.cloned.1.call-start = ((), (), s32[]{:S(2)}) async-start(), calls=%async_computation.10 | async-start | bytes 21233664 | tf_op jit(solution)/shard_map/reduce_scatter | solution.py:117
  117.1 294.1 %all-gather.6.cloned.1.call-start = ((), (), s32[]{:S(2)}) async-start(), calls=%async_computation.12 | async-start | bytes 3538944 | tf_op jit(solution)/shard_map/all_gather | solution.py:106
  118.0 166.3 %copy-start.49 = (pred[4,4]{1,0:T(4,128)(4,1)}, pred[4,4]{1,0:T(4,128)(4,1)S(1)}, u32[]{:S(2)}) copy-start(pred[4,4]{1,0:T(4,128)(4,1)S(1)} %iota_compare_fusion.6) | copy-start | bytes 52
  371.1 40.0 %copy-start.56 = (bf16[384,768]{1,0:T(8,128)(2,1)S(1)}, bf16[384,768]{1,0:T(8,128)(2,1)}, u32[]{:S(2)}) copy-start(bf16[384,768]{1,0:T(8,128)(2,1)} %param.23) | copy-start | bytes 1769476
  374.9 206.3 %reduce-scatter.15.cloned.1.call-start = ((), (), s32[]{:S(2)}) async-start(), calls=%async_computation.13 | async-start | bytes 5898240 | tf_op jit(solution)/shard_map/reduce_scatter | solution.py:100
  417.6 269.9 %reduce-scatter.23.cloned.1.call-start = ((), (), s32[]{:S(2)}) async-start(), calls=%async_computation.18 | async-start | bytes 9437184 | tf_op jit(solution)/shard_map/reduce_scatter | solution.py:110
  418.8 52.5 %collective-permute-start.6 = (bf16[768,768]{1,0:T(8,128)(2,1)S(1)}, bf16[768,768]{1,0:T(8,128)(2,1)S(1)}, u32[]{:S(2)}, u32[]{:S(2)}) collective-permute-start(bf16[768,768]{1,0:T(8,128)(2,1)S(1)} %copy-done.11), channel_id=1, source_target_pairs={{0,1},{1,2},{2,3},{3,0},{4,5},{5,6},{6,7},{7,4},{8,9},{9,10},{10,1... | collective-permute-start | bytes 3538952 | tf_op jit(solution)/shard_map/ppermute | solution.py:24
  420.3 107.2 %collective-permute-start.7 = (bf16[768,768]{1,0:T(8,128)(2,1)S(1)}, bf16[768,768]{1,0:T(8,128)(2,1)S(1)}, u32[]{:S(2)}, u32[]{:S(2)}) collective-permute-start(bf16[768,768]{1,0:T(8,128)(2,1)S(1)} %copy-done.11), channel_id=1, source_target_pairs={{0,3},{1,0},{2,1},{3,2},{4,7},{5,4},{6,5},{7,6},{8,11},{9,8},{10,9... | collective-permute-start | bytes 3538952 | tf_op jit(solution)/shard_map/ppermute | solution.py:29
  471.4 100.1 %collective-permute-start.8 = (bf16[768,768]{1,0:T(8,128)(2,1)S(1)}, bf16[768,768]{1,0:T(8,128)(2,1)S(1)}, u32[]{:S(2)}, u32[]{:S(2)}) collective-permute-start(bf16[768,768]{1,0:T(8,128)(2,1)S(1)} %collective-permute-done.6), channel_id=1, source_target_pairs={{0,1},{1,2},{2,3},{3,0},{4,5},{5,6},{6,7},{7,4},{8,9},{9,10},{10,1... | collective-permute-start | bytes 3538952 | tf_op jit(solution)/shard_map/ppermute | solution.py:24
  502.8 70.9 %copy-start.54 = (bf16[1024,768]{1,0:T(8,128)(2,1)S(1)}, bf16[1024,768]{1,0:T(8,128)(2,1)}, u32[]{:S(2)}) copy-start(bf16[1024,768]{1,0:T(8,128)(2,1)} %param.27) | copy-start | bytes 4718596
  581.1 8.3 copy-start.25
  581.1 238.8 %reduce-scatter.19.cloned.1.call-start = ((), (), s32[]{:S(2)}) async-start(), calls=%async_computation.15 | async-start | bytes 18874368 | tf_op jit(solution)/shard_map/reduce_scatter | solution.py:118
  589.1 655.3 %copy-start.23 = (f32[768]{0:T(1024)}, f32[768]{0:T(1024)S(1)}, u32[]{:S(2)}) copy-start(f32[768]{0:T(1024)S(1)} %get-tuple-element.306) | copy-start | bytes 9220
  589.1 655.3 %copy-start.31 = (f32[768]{0:T(1024)}, f32[768]{0:T(1024)S(1)}, u32[]{:S(2)}) copy-start(f32[768]{0:T(1024)S(1)} %get-tuple-element.305) | copy-start | bytes 9220
  590.8 30.8 %collective-permute-start.3 = (bf16[768,768]{1,0:T(8,128)(2,1)S(1)}, bf16[768,768]{1,0:T(8,128)(2,1)S(1)}, u32[]{:S(2)}, u32[]{:S(2)}) collective-permute-start(bf16[768,768]{1,0:T(8,128)(2,1)S(1)} %get-tuple-element.284), channel_id=1, source_target_pairs={{0,1},{1,2},{2,3},{3,0},{4,5},{5,6},{6,7},{7,4},{8,9},{9,10},{10,1... | collective-permute-start | bytes 3538952 | tf_op jit(solution)/shard_map/ppermute | solution.py:24
  591.5 53.6 %collective-permute-start.4 = (bf16[768,768]{1,0:T(8,128)(2,1)S(1)}, bf16[768,768]{1,0:T(8,128)(2,1)S(1)}, u32[]{:S(2)}, u32[]{:S(2)}) collective-permute-start(bf16[768,768]{1,0:T(8,128)(2,1)S(1)} %get-tuple-element.284), channel_id=1, source_target_pairs={{0,3},{1,0},{2,1},{3,2},{4,7},{5,4},{6,5},{7,6},{8,11},{9,8},{10,9... | collective-permute-start | bytes 3538952 | tf_op jit(solution)/shard_map/ppermute | solution.py:29
  621.5 45.1 %collective-permute-start.5 = (bf16[768,768]{1,0:T(8,128)(2,1)S(1)}, bf16[768,768]{1,0:T(8,128)(2,1)S(1)}, u32[]{:S(2)}, u32[]{:S(2)}) collective-permute-start(bf16[768,768]{1,0:T(8,128)(2,1)S(1)} %collective-permute-done.3), channel_id=1, source_target_pairs={{0,1},{1,2},{2,3},{3,0},{4,5},{5,6},{6,7},{7,4},{8,9},{9,10},{10,1... | collective-permute-start | bytes 3538952 | tf_op jit(solution)/shard_map/ppermute | solution.py:24
  641.6 27.2 %copy-start.53 = (bf16[768,1024]{1,0:T(8,128)(2,1)S(1)}, bf16[768,1024]{1,0:T(8,128)(2,1)}, u32[]{:S(2)}) copy-start(bf16[768,1024]{1,0:T(8,128)(2,1)} %param.26) | copy-start | bytes 4718596
  676.9 289.9 %reduce-scatter.17.cloned.1.call-start = ((), (), s32[]{:S(2)}) async-start(), calls=%async_computation.14 | async-start | bytes 18874368 | tf_op jit(solution)/shard_map/reduce_scatter | solution.py:117
  687.4 369.9 %all-gather.10.cloned.1.call-start = ((), (), s32[]{:S(2)}) async-start(), calls=%async_computation.19 | async-start | bytes 9437184 | tf_op jit(solution)/shard_map/all_gather | solution.py:124
  976.7 163.2 %all-gather.12.cloned.1.call-start = ((), (), s32[]{:S(2)}) async-start(), calls=%async_computation.20 | async-start | bytes 9437184 | tf_op jit(solution)/shard_map/all_gather | solution.py:125
  977.5 258.4 %reduce-scatter.25.cloned.1.call-start = ((), (), s32[]{:S(2)}) async-start(), calls=%async_computation.21 | async-start | bytes 5898240 | tf_op jit(solution)/shard_map/reduce_scatter | solution.py:100
  1150.4 215.5 %reduce-scatter.27.cloned.1.call-start = ((), (), s32[]{:S(2)}) async-start(), calls=%async_computation.22 | async-start | bytes 3538944 | tf_op jit(solution)/shard_map/reduce_scatter | solution.py:110
  1247.2 30.8 %collective-permute-start.9 = (bf16[768,768]{1,0:T(8,128)(2,1)S(1)}, bf16[768,768]{1,0:T(8,128)(2,1)S(1)}, u32[]{:S(2)}, u32[]{:S(2)}) collective-permute-start(bf16[768,768]{1,0:T(8,128)(2,1)S(1)} %get-tuple-element.282), channel_id=1, source_target_pairs={{0,1},{1,2},{2,3},{3,0},{4,5},{5,6},{6,7},{7,4},{8,9},{9,10},{10,1... | collective-permute-start | bytes 3538952 | tf_op jit(solution)/shard_map/ppermute | solution.py:24
  1248.7 53.8 %collective-permute-start.10 = (bf16[768,768]{1,0:T(8,128)(2,1)S(1)}, bf16[768,768]{1,0:T(8,128)(2,1)S(1)}, u32[]{:S(2)}, u32[]{:S(2)}) collective-permute-start(bf16[768,768]{1,0:T(8,128)(2,1)S(1)} %get-tuple-element.282), channel_id=1, source_target_pairs={{0,3},{1,0},{2,1},{3,2},{4,7},{5,4},{6,5},{7,6},{8,11},{9,8},{10,9... | collective-permute-start | bytes 3538952 | tf_op jit(solution)/shard_map/ppermute | solution.py:29
  1278.0 48.3 %collective-permute-start.11 = (bf16[768,768]{1,0:T(8,128)(2,1)S(1)}, bf16[768,768]{1,0:T(8,128)(2,1)S(1)}, u32[]{:S(2)}, u32[]{:S(2)}) collective-permute-start(bf16[768,768]{1,0:T(8,128)(2,1)S(1)} %collective-permute-done.9), channel_id=1, source_target_pairs={{0,1},{1,2},{2,3},{3,0},{4,5},{5,6},{6,7},{7,4},{8,9},{9,10},{10,1... | collective-permute-start | bytes 3538952 | tf_op jit(solution)/shard_map/ppermute | solution.py:24
  1299.6 28.9 %copy-start.57 = (bf16[384,768]{1,0:T(8,128)(2,1)S(1)}, bf16[384,768]{1,0:T(8,128)(2,1)}, u32[]{:S(2)}) copy-start(bf16[384,768]{1,0:T(8,128)(2,1)} %param.23) | copy-start | bytes 1769476
  1332.4 35.9 %copy-start.7 = (bf16[1536,6,64]{0,2,1:T(8,128)(2,1)S(1)}, bf16[1536,6,64]{0,2,1:T(8,128)(2,1)}, u32[]{:S(2)}) copy-start(bf16[1536,6,64]{0,2,1:T(8,128)(2,1)} %get-tuple-element.602) | copy-start | bytes 3538948
  1332.4 269.9 %all-gather.8.cloned.1.call-start = ((), (), s32[]{:S(2)}) async-start(), calls=%async_computation.16 | async-start | bytes 9437184 | tf_op jit(solution)/shard_map/all_gather | solution.py:106
  1333.0 339.1 %all-gather.14.cloned.1.call-start = ((), (), s32[]{:S(2)}) async-start(), calls=%async_computation.23 | async-start | bytes 10616832 | tf_op jit(solution)/shard_map/all_gather | solution.py:124
  1373.2 10.8 copy-start.21
  1399.2 20.6 %copy-start.1 = (f32[6,512,1536]{2,1,0:T(8,128)S(1)}, f32[6,512,1536]{2,1,0:T(8,128)}, u32[]{:S(2)}) copy-start(f32[6,512,1536]{2,1,0:T(8,128)} %get-tuple-element.470) | copy-start | bytes 56623108 | tf_op jit(solution)/shard_map/while
  1424.1 7.8 copy-start.2
  1441.0 9.2 copy-start.21
  1465.3 20.6 %copy-start.1 = (f32[6,512,1536]{2,1,0:T(8,128)S(1)}, f32[6,512,1536]{2,1,0:T(8,128)}, u32[]{:S(2)}) copy-start(f32[6,512,1536]{2,1,0:T(8,128)} %get-tuple-element.470) | copy-start | bytes 56623108 | tf_op jit(solution)/shard_map/while
  1491.1 7.8 copy-start.2
  1508.7 9.2 copy-start.21
  1533.1 20.6 %copy-start.1 = (f32[6,512,1536]{2,1,0:T(8,128)S(1)}, f32[6,512,1536]{2,1,0:T(8,128)}, u32[]{:S(2)}) copy-start(f32[6,512,1536]{2,1,0:T(8,128)} %get-tuple-element.470) | copy-start | bytes 56623108 | tf_op jit(solution)/shard_map/while
  1558.9 7.8 copy-start.2
  1582.4 234.5 %all-reduce.8.cloned.1.call-start = ((), (), s32[]{:S(2)}) async-start(), calls=%async_computation.25 | async-start | bytes 14155776 | tf_op jit(solution)/shard_map/psum | solution.py:293
  1602.4 9.6 copy-start.52
  1683.3 8.2 copy-start.41
  1683.3 8.4 copy-start.22
  1683.3 8.4 copy-start.48
  1683.3 221.2 %reduce-scatter.29.cloned.1.call-start = ((), (), s32[]{:S(2)}) async-start(), calls=%async_computation.24 | async-start | bytes 5898240 | tf_op jit(solution)/shard_map/reduce_scatter | solution.py:100
  1696.3 8.8 copy-start.30
  1708.7 286.0 %reduce-scatter.21.cloned.1.call-start = ((), (), s32[]{:S(2)}) async-start(), calls=%async_computation.17 | async-start | bytes 5898240 | tf_op jit(solution)/shard_map/reduce_scatter | solution.py:100
  1826.8 77.7 %copy-start.6 = (bf16[768,768]{1,0:T(8,128)(2,1)S(1)}, bf16[768,768]{1,0:T(8,128)(2,1)}, u32[]{:S(2)}) copy-start(bf16[768,768]{1,0:T(8,128)(2,1)} %param.18) | copy-start | bytes 3538948
  1826.8 77.7 %copy-start.28 = (f32[768]{0:T(1024)S(1)}, f32[768]{0:T(1024)}, u32[]{:S(2)}) copy-start(f32[768]{0:T(1024)} %copy-done.27) | copy-start | bytes 9220
  1826.8 77.7 %copy-start.38 = (f32[768]{0:T(1024)S(1)}, f32[768]{0:T(1024)}, u32[]{:S(2)}) copy-start(f32[768]{0:T(1024)} %param.19) | copy-start | bytes 9220
  1827.0 79.8 %copy-start.45 = (f32[768]{0:T(1024)S(1)}, f32[768]{0:T(1024)}, u32[]{:S(2)}) copy-start(f32[768]{0:T(1024)} %get-tuple-element.217) | copy-start | bytes 9220
  1827.0 167.6 %copy-start.24 = (f32[768]{0:T(1024)S(1)}, f32[768]{0:T(1024)}, u32[]{:S(2)}) copy-start(f32[768]{0:T(1024)} %copy-done.23) | copy-start | bytes 9220
  1827.0 167.6 %copy-start.26 = (f32[768]{0:T(1024)S(1)}, f32[768]{0:T(1024)}, u32[]{:S(2)}) copy-start(f32[768]{0:T(1024)} %param.24) | copy-start | bytes 9220
  1827.0 167.6 %copy-start.32 = (f32[768]{0:T(1024)S(1)}, f32[768]{0:T(1024)}, u32[]{:S(2)}) copy-start(f32[768]{0:T(1024)} %copy-done.31) | copy-start | bytes 9220
  1827.0 167.6 %copy-start.34 = (f32[768]{0:T(1024)S(1)}, f32[768]{0:T(1024)}, u32[]{:S(2)}) copy-start(f32[768]{0:T(1024)} %copy-done.33) | copy-start | bytes 9220
  1827.0 167.6 %copy-start.44 = (f32[768]{0:T(1024)S(1)}, f32[768]{0:T(1024)}, u32[]{:S(2)}) copy-start(f32[768]{0:T(1024)} %get-tuple-element.303) | copy-start | bytes 9220
  (30 other events, 91.1 us)
Sparse Core Ops, SparseCore 0:
  106.0 9.3 reduce-scatter.12
  117.7 161.4 reduce-scatter.10
  375.0 36.0 all-gather.5
  417.7 157.8 reduce-scatter.14
  581.2 76.4 reduce-scatter.22
  677.0 142.8 reduce-scatter.18
  822.3 144.4 reduce-scatter.16
  976.8 80.3 all-gather.9
  1059.5 80.3 all-gather.11
  1150.5 85.2 reduce-scatter.24
  1332.5 33.3 reduce-scatter.26
  1367.9 80.3 all-gather.7
  1582.5 89.5 all-gather.13
  1683.5 133.3 all-reduce.7
  1819.0 85.4 reduce-scatter.28
  1906.6 87.9 reduce-scatter.20
